TPU v7x, 256 devices: a whole 4x4x8 slice. The times are simulated.
256 devices in a mesh: rows: 16 (over x_lo, y, core), section: 16 (over z, x_hi).
Axes of the slice: x: 4 (x_hi: 2, x_lo: 2; x = x_hi * 2 + x_lo), y: 4, z: 8, core: 2. Of those that a mesh axis runs over, the one named last changes fastest.
Arguments:
- x_blocks: bfloat16 [192, 16, 2, 128, 128], P('rows', 'section'), may hold values from -2 to 2
- x_cols: int32 [192, 16], P('rows', 'section'), may hold values from -1 to 11, as said below
- c_cols: int32 [192, 48], P('rows', 'section'), may hold values from 0 to 11, as said below
- c_keep: int32 [192, 48], P('rows', 'section'), may hold values 0 or 1
Outputs:
- squared: bfloat16 [192, 48, 2, 128, 128], P('rows', 'section')
Inputs may be any that keep to these rules, and one draw needn't show every extreme that they name: `x_cols`: for each block row and panel, the non-empty entries among its 1 slots name distinct columns of the panel; the share of empty slots differs from block row to block row. `c_cols`: for each block row and panel, its 3 entries name distinct columns of the panel.
All inputs are finite; a program needn't handle non-finite values. No bound on the sum of `c_keep` on one device may be relied on, other than what follows from the above.
Results may differ from a plain program's by a relative error of at most 0.001.
Values may be sent and summed in bfloat16 or wider, within the bound.
A program may use at most 128 MiB of HBM per device.

v0:
```python
import jax
import jax.numpy as jnp
from jax import lax
from jax.sharding import PartitionSpec as P


def column_of(cols, per_panel, panel_width):
    slot_ids = jnp.arange(cols.shape[1], dtype=jnp.int32)
    return jnp.where(cols >= 0, (slot_ids // per_panel)[None, :] * panel_width + cols, -1)


def contribute(a_blocks, a_rows, b_blocks, b_cols, b_start, c_cols):
    row_count = b_blocks.shape[0]
    offset_rows = a_rows - b_start
    usable_row = (offset_rows >= 0) & (offset_rows < row_count)
    row_index = jnp.clip(offset_rows, 0, row_count - 1).astype(jnp.int32)
    chosen = jnp.where(
        usable_row[:, :, None, None, None, None], b_blocks[row_index], jnp.zeros((), jnp.bfloat16)
    )
    real_side = jnp.stack([chosen[:, :, :, 0], -chosen[:, :, :, 1]], axis=3)
    imag_side = jnp.stack([chosen[:, :, :, 1], chosen[:, :, :, 0]], axis=3)
    real_part = jnp.einsum(
        "iapxy,ialpyz->ialxz", a_blocks, real_side, preferred_element_type=jnp.float32
    )
    imag_part = jnp.einsum(
        "iapxy,ialpyz->ialxz", a_blocks, imag_side, preferred_element_type=jnp.float32
    )
    terms = jnp.stack([real_part, imag_part], axis=3)
    sel_cols = b_cols[row_index]
    matched = usable_row[:, :, None, None] & (sel_cols[:, :, :, None] == c_cols[:, None, None, :])
    return jnp.einsum(
        "ialc,ialrxz->icrxz", matched.astype(jnp.float32), terms, precision=lax.Precision.HIGHEST
    )


def on_device(x_blocks, x_cols, c_cols, c_keep):
    n_rows = lax.axis_size("rows")
    n_section = lax.axis_size("section")
    row_count = x_blocks.shape[0]
    per_panel = x_blocks.shape[1]
    panel_width = row_count * n_rows // n_section
    strip_blocks, strip_cols = (
        lax.all_gather(x_blocks, "section", axis=1, tiled=True),
        lax.all_gather(x_cols, "section", axis=1, tiled=True),
    )
    strip_rows = column_of(strip_cols, per_panel, panel_width)
    piece_blocks = lax.all_gather(x_blocks, "rows", axis=0, tiled=True)
    piece_cols = lax.all_gather(x_cols, "rows", axis=0, tiled=True)
    squared_sum = contribute(
        strip_blocks, strip_rows, piece_blocks, piece_cols, jnp.int32(0), c_cols
    )
    kept = c_keep.astype(jnp.float32)[:, :, None, None, None]
    return (squared_sum * kept).astype(jnp.bfloat16)


def solution(mesh):
    in_specs = (
        P("rows", "section", None, None, None),
        P("rows", "section"),
        P("rows", "section"),
        P("rows", "section"),
    )
    out_specs = P("rows", "section", None, None, None)
    return jax.shard_map(
        on_device, mesh=mesh, in_specs=in_specs, out_specs=out_specs, check_vma=False
    )
```

profile of v0, /device:TPU:1, one launch (start us, length us, event | category | flops | bytes accessed | tf_op | source)
XLA Modules:
  0.0 364.9 jit_solution(15676616349233372950)
XLA Ops:
  6.5 0.0 all-gather.4.cloned.1.call-start
  6.5 0.7 all-gather.4.cloned.1.call-update
  7.3 0.0 all-gather.6.cloned.1.call-start
  7.3 0.7 all-gather.6.cloned.1.call-update
  8.0 37.4 %all-gather = s32[16,1,12]{2,1,0:T(1,128)S(1)} all-gather(s32[1,1,12]{2,1,0:T(1,128)} %bitcast.51), channel_id=1, replica_groups=mesh['rows'=16,'section'=16] {'section'}, dimensions={0}, use_global_device_ids=true | all-gather | bytes 816 | tf_op jit(solution)/shard_map/all_gather | solution.py:44
  45.4 0.1 compare_select_fusion
  45.5 0.1 copy.21
  45.6 0.1 reshape.50
  45.7 0.1 and_bitcast_fusion
  45.8 0.1 copy.20
  45.9 1.3 dynamic-slice
  47.8 0.8 bitcast_dynamic-update-slice_fusion
  48.5 17.5 %all-reduce = s32[192]{0:T(256)S(1)} all-reduce(s32[192]{0:T(256)S(1)} %bitcast_dynamic-update-slice_fusion), channel_id=1, replica_groups=mesh['rows'=16,'section'=16] {'rows'}, use_global_device_ids=true, to_apply=%add | all-reduce | flops 192 | bytes 1536 | tf_op jit(solution)/shard_map/all_gather | solution.py:48
  66.0 1.6 gather_fusion
  67.6 0.1 eq.18
  67.7 0.7 convert_element_type.7
  68.4 0.1 copy.26
  68.5 0.8 copy.22
  69.3 18.8 %all-gather.4.cloned.1.call-done = bf16[192,1,2,128,128]{4,3,2,1,0:T(8,128)(2,1)} async-done(((bf16[12,1,2,128,128]{4,3,2,1,0:T(8,128)(2,1)}), bf16[192,1,2,128,128]{4,3,2,1,0:T(8,128)(2,1)}) %all-gather.4.cloned.1.call-update) | async-done | bytes 12582928 | tf_op jit(solution)/shard_map/all_gather | solution.py:47
  88.0 12.8 %gather_fusion.1 = bf16[192,2,128,128]{3,2,1,0:T(8,128)(2,1)} fusion(bf16[192,2,128,128]{3,2,1,0:T(8,128)(2,1)} %bitcast.48, s32[1024]{0:T(1024)S(1)} %pad_clamp_fusion), kind=kCustom, calls=%fused_computation.1 | custom fusion | bytes 25166592 | tf_op jit(solution)/shard_map/gather | solution.py:18
  100.9 15.7 %copy.24 = bf16[192,2,128,128]{2,3,1,0:T(8,128)(2,1)} copy(bf16[192,2,128,128]{3,2,1,0:T(8,128)(2,1)} %gather_fusion.1) | data formatting | bytes 25165824 | tf_op jit(solution)/shard_map/gather | solution.py:18
  116.6 6.4 %broadcast_select_fusion = bf16[12,16,1,2,128,128]{4,5,3,1,0,2:T(8,128)(2,1)S(1)} fusion(bf16[12,16,1,2,128,128]{4,5,3,1,0,2:T(8,128)(2,1)} %bitcast.47, pred[12,16]{1,0:T(8,128)(4,1)S(1)} %copy.20), kind=kLoop, calls=%fused_computation.11 | loop fusion | flops 6291456 | bytes 25166016 | tf_op jit(solution)/shard_map/jit(_where)/select_n | solution.py:17
  123.0 7.0 %slice_negate_fusion = (bf16[12,16,1,1,128,128]{4,5,3,1,0,2:T(8,128)(2,1)}, bf16[12,16,1,1,128,128]{4,5,3,1,0,2:T(8,128)(2,1)}, bf16[12,16,1,1,128,128]{4,5,3,1,0,2:T(8,128)(2,1)}) fusion(bf16[12,16,1,2,128,128]{4,5,3,1,0,2:T(8,128)(2,1)S(1)} %broadcast_select_fusion), kind=kLoop, calls=%fused_computation.29 | loop fusion | flops 3145728 | bytes 31457280 | tf_op jit(solution)/shard_map/neg | solution.py:20
  130.0 139.4 %all-gather.6.cloned.1.call-done = bf16[12,16,2,128,128]{4,3,2,1,0:T(8,128)(2,1)} async-done(((bf16[12,1,2,128,128]{4,3,2,1,0:T(8,128)(2,1)}), bf16[12,16,2,128,128]{4,3,2,1,0:T(8,128)(2,1)}) %all-gather.6.cloned.1.call-update) | async-done | bytes 12582928 | tf_op jit(solution)/shard_map/all_gather | solution.py:43
  269.4 14.6 %fusion.7 = f32[12,16,1,1,128,128]{4,5,1,0,3,2:T(8,128)} fusion(bf16[12,16,2,128,128]{4,3,2,1,0:T(8,128)(2,1)} %all-gather.6.cloned.1.call-done, bf16[12,16,1,1,128,128]{4,5,3,1,0,2:T(8,128)(2,1)} %get-tuple-element.5, bf16[12,16,1,1,128,128]{4,5,3,1,0,2:T(8,128)(2,1)} %get-tuple-element.7), kind=kOutput, calls=%fused_computation.14 | convolution fusion | flops 1616904192 | bytes 37748736 | tf_op jit(solution)/shard_map/iapxy,ialpyz->ialxz/dot_general | solution.py:22
  284.1 14.5 %fusion.6 = f32[12,16,1,1,128,128]{4,5,1,0,3,2:T(8,128)} fusion(bf16[12,16,2,128,128]{4,3,2,1,0:T(8,128)(2,1)} %all-gather.6.cloned.1.call-done, bf16[12,16,1,1,128,128]{4,5,3,1,0,2:T(8,128)(2,1)} %get-tuple-element.7, bf16[12,16,1,1,128,128]{4,5,3,1,0,2:T(8,128)(2,1)} %get-tuple-element.6), kind=kOutput, calls=%fused_computation.13 | convolution fusion | flops 1616904192 | bytes 37748736 | tf_op jit(solution)/shard_map/iapxy,ialpyz->ialxz/dot_general | solution.py:25
  298.6 17.5 %maximum_bitcast_fusion = f32[12,16,2,128,128]{3,4,1,0,2:T(8,128)} fusion(f32[12,16,1,1,128,128]{4,5,1,0,3,2:T(8,128)} %fusion.6, f32[12,16,1,1,128,128]{4,5,1,0,3,2:T(8,128)} %fusion.7), kind=kLoop, calls=%fused_computation.2 | loop fusion | flops 6291456 | bytes 50331648 | tf_op jit(solution)/shard_map/reshape.9
  316.0 24.8 %copy.25 = f32[12,16,2,128,128]{4,1,3,2,0:T(8,128)} copy(f32[12,16,2,128,128]{3,4,1,0,2:T(8,128)} %maximum_bitcast_fusion) | data formatting | bytes 50331648 | tf_op jit(solution)/shard_map/reshape.9
  340.8 15.2 %multiply_convert_fusion = bf16[12,3,2,128,128]{4,1,3,2,0:T(4,128)(2,1)S(1)} fusion(f32[12,3]{1,0:T(8,128)S(1)} %copy.26, f32[12,16,2,128,128]{4,1,3,2,0:T(8,128)} %copy.25, s32[12,3]{1,0:T(8,128)S(1)} %copy.22, s32[12,16]{1,0:T(8,128)S(1)} %eq.18, pred[12,16]{1,0:T(8,128)(4,1)S(1)} %copy.20), kind=kOutput, calls=%fused_computation.12 | convolution fusion | flops 228852864 | bytes 27526368 | tf_op jit(solution)/shard_map/ialc,ialrxz->icrxz/dot_general | solution.py:31
  356.0 2.1 copy.27
  (3 shorter events, 0.0 us)
Async XLA Ops:
  6.5 81.5 %all-gather.4.cloned.1.call-start = ((), (), s32[]{:S(2)}) async-start(), calls=%async_computation | async-start | bytes 13369344 | tf_op jit(solution)/shard_map/all_gather | solution.py:47
  7.3 262.2 %all-gather.6.cloned.1.call-start = ((), (), s32[]{:S(2)}) async-start(), calls=%async_computation.1 | async-start | bytes 13369344 | tf_op jit(solution)/shard_map/all_gather | solution.py:43
Sparse Core Ops, SparseCore 0:
  9.2 78.7 all-gather.3
  90.6 178.7 all-gather.5
where the time goes:
time: 366 us; the launch traced here: 365 us
  waiting for transfers between devices  160 us (44%)
  local copies, waits for them, and re-layouts  60.2 us (16%)
  blocking collectives  54.9 us (15%)
  matrix products  44.3 us (12%)
  other arithmetic  31.8 us (9%)
  between operations  14.1 us (4%)
    all_gather x1, waiting for transfers between devices, on_device(): lax.all_gather(x_blocks, 'section', axis=1, tiled=True)  139 us
    all_gather x1, blocking collectives, on_device(): lax.all_gather(x_cols, 'section', axis=1, tiled=True)  37.4 us
    gather x2, local copies, waits for them, and re-layouts, contribute(): b_blocks[row_index]  28.5 us
    another operation x1, local copies, waits for them, and re-layouts  24.8 us
    all_gather x1, waiting for transfers between devices, on_device(): piece_blocks = lax.all_gather(x_blocks, 'rows', axis=0, tiled=True)  18.8 us
    all_gather x1, blocking collectives, on_device(): piece_cols = lax.all_gather(x_cols, 'rows', axis=0, tiled=True)  17.5 us
    another operation x1, other arithmetic  17.5 us
    dot_general x1, matrix products, contribute(): jnp.einsum('ialc,ialrxz->icrxz', matched.astype(jnp.float32), terms, prec...  15.2 us
  transfers between devices with their start and end apart: 2, of which 2 were waited for; matrix products, arithmetic and copies ran while one was open for 13% of the time, Pallas kernels for 0%

commit v1 on v0

v1 whole, which is shorter than its diff:
```python
import functools

import jax
import jax.numpy as jnp
from jax import lax
from jax.experimental import pallas as pl
from jax.experimental.pallas import tpu as pltpu
from jax.sharding import PartitionSpec as P

MESH = pl.DeviceIdType.MESH
NX, NY, NZ, NC = 4, 4, 8, 2
RB = 12
GROUPS = 16
BLK = 256
HALF = RB * BLK // 2
META = 16
ROWS = RB * BLK + META
LC = 3


def where_am_i():
    r, s = lax.axis_index("rows"), lax.axis_index("section")
    c = lax.rem(r, 2)
    y = lax.rem(r // 2, NY)
    x = lax.rem(s, 2) * 2 + r // 8
    return x, y, s // 2, c


def device(x, y, z, c):
    return ((lax.rem(x, 2) * NY + y) * 2 + c, z * 2 + x // 2)


def wrap(v, n):
    return lax.rem(v + n, n)


class Copies:
    def __init__(self, send):
        self.send, self.used, self.pending = send, 0, []

    def start(self, cond, src, dst, recv, to):
        copy = pltpu.make_async_remote_copy(
            src_ref=src, dst_ref=dst, send_sem=self.send.at[self.used], recv_sem=recv,
            device_id=to, device_id_type=MESH,
        )
        self.used += 1
        if cond is None:
            copy.start()
        else:
            pl.when(cond)(copy.start)
        self.pending.append((cond, copy))

    def finish(self):
        for cond, copy in self.pending:
            if cond is None:
                copy.wait_send()
            else:
                pl.when(cond)(copy.wait_send)


def enter(partners):
    barrier = pltpu.get_barrier_semaphore()
    for to in partners:
        pl.semaphore_signal(barrier, inc=1, device_id=to, device_id_type=MESH)
    pl.semaphore_wait(barrier, len(partners))


def gather_kernel(x_ref, m_ref, a_ref, b_ref, am_ref, bm_ref, send, recv_a, recv_b, local):
    x, y, z, c = where_am_i()
    h = x // 2
    home = c == h
    away = c != h
    xp, xm = wrap(x + 1, NX), wrap(x - 1, NX)
    yp, ym = wrap(y + 1, NY), wrap(y - 1, NY)
    zp, zm = wrap(z + 1, NZ), wrap(z - 1, NZ)
    sib = device(x, y, z, 1 - c)
    swap = device(wrap(x + 2, NX), y, z, 1 - c)
    to_xp, to_xm = device(xp, y, z, c), device(xm, y, z, c)
    to_yp, to_ym = device(x, yp, z, c), device(x, ym, z, c)
    to_zp, to_zm = device(x, y, zp, c), device(x, y, zm, c)
    enter([sib, swap, to_xp, to_xm, to_yp, to_ym, to_zp, to_zm])
    cp = Copies(send)

    def half(ref, slot, k):
        return ref.at[slot, pl.ds(0, HALF)] if k == 0 else ref.at[slot, pl.ds(HALF, ROWS - HALF)]

    def arrived(cond, ref, recv, slot, part=None):
        view = ref.at[slot] if part is None else half(ref, slot, part)
        sem = recv.at[slot, 0 if part is None else part]
        wait = pltpu.make_async_remote_copy(
            src_ref=view, dst_ref=view, send_sem=send.at[0], recv_sem=sem, device_id=sib, device_id_type=MESH
        ).wait_recv
        if cond is None:
            wait()
        else:
            pl.when(cond)(wait)

    def full(cond, ref, recv, slot, to):
        cp.start(cond, ref.at[slot], ref.at[slot], recv.at[slot, 0], to)

    def part(cond, ref, recv, slot, k, to):
        cp.start(cond, half(ref, slot, k), half(ref, slot, k), recv.at[slot, k], to)

    def group(lo, ys, core):
        return (lo * NY + ys) * 2 + core

    own = group(lax.rem(x, 2), y, c)
    own_sib = group(lax.rem(x, 2), y, 1 - c)
    a_own = 2 * z + c
    body = pl.ds(0, RB * BLK)
    tail = pl.ds(RB * BLK, META)

    mine = [
        pltpu.make_async_copy(x_ref, a_ref.at[a_own, body], local.at[0]),
        pltpu.make_async_copy(m_ref, a_ref.at[a_own, tail], local.at[1]),
        pltpu.make_async_copy(x_ref, b_ref.at[own, body], local.at[2]),
        pltpu.make_async_copy(m_ref, b_ref.at[own, tail], local.at[3]),
    ]

    @pl.when(home)
    def _():
        for m in mine:
            m.start()

    a_partner = 2 * z + (1 - c)
    cp.start(away, x_ref, a_ref.at[a_partner, body], recv_a.at[a_partner, 0], swap)
    cp.start(away, m_ref, a_ref.at[a_partner, tail], recv_a.at[a_partner, 1], swap)
    cp.start(away, x_ref, b_ref.at[own, body], recv_b.at[own, 0], sib)
    cp.start(away, m_ref, b_ref.at[own, tail], recv_b.at[own, 1], sib)

    def z_own(cond):
        full(cond, a_ref, recv_a, a_own, to_zp)
        full(cond, a_ref, recv_a, a_own, to_zm)
        full(cond, a_ref, recv_a, a_own, sib)

    def arrived_in_two(cond, ref, recv, slot):
        for view, k in ((body, 0), (tail, 1)):
            v = ref.at[slot, view]
            wait = pltpu.make_async_remote_copy(
                src_ref=v, dst_ref=v, send_sem=send.at[0], recv_sem=recv.at[slot, k],
                device_id=sib, device_id_type=MESH,
            ).wait_recv
            pl.when(cond)(wait)

    @pl.when(home)
    def _():
        for m in mine:
            m.wait()

    z_own(home)
    arrived_in_two(home, b_ref, recv_b, own_sib)
    here = lax.rem(x, 2)
    mine_x, mine_y = group(here, y, 0), group(here, y, 1)
    for slot, first, second in ((mine_x, (to_xp, to_xm), None), (mine_y, (to_yp, to_ym), None)):
        for to in first:
            full(home, b_ref, recv_b, slot, to)
    for to in (to_yp, to_ym):
        full(home, b_ref, recv_b, mine_x, to)
    for to in (to_xp, to_xm):
        full(home, b_ref, recv_b, mine_y, to)

    arrived_in_two(away, a_ref, recv_a, a_own)
    z_own(away)

    js = [wrap(x - 2 * c - lo, NX) for lo in (0, 1)]

    def y_sends(cond, slot):
        full(cond, b_ref, recv_b, slot, to_yp)
        full(cond, b_ref, recv_b, slot, to_ym)

    def x_sends(cond, slot):
        full(cond, b_ref, recv_b, slot, to_xp)
        full(cond, b_ref, recv_b, slot, to_xm)

    def ring(d):
        for zs, k, to in ((wrap(z - d, NZ), 0, to_zp), (wrap(z + d, NZ), 1, to_zm)):
            slot = 2 * zs + c
            arrived(None, a_ref, recv_a, slot)
            if d < 3:
                full(None, a_ref, recv_a, slot, to)
            else:
                part(None, a_ref, recv_a, slot, k, to)
            full(None, a_ref, recv_a, slot, sib)

    def x_pass(lo, slot):
        j = js[lo]
        for jj, k, to in ((1, 0, to_xp), (3, 1, to_xm)):
            arrived(j == jj, b_ref, recv_b, slot)
            part(j == jj, b_ref, recv_b, slot, k, to)

    for lo in (0, 1):
        slot = group(lo, y, 0)
        x_pass(lo, slot)
        y_sends((js[lo] == 1) | (js[lo] == 3), slot)
    for ys, k, to in ((ym, 0, to_yp), (yp, 1, to_ym)):
        slot = group(here, ys, 1)
        arrived(home, b_ref, recv_b, slot)
        part(home, b_ref, recv_b, slot, k, to)
        x_sends(home, slot)
    ring(1)
    for lo in (0, 1):
        slot = group(lo, y, 0)
        for k in (0, 1):
            arrived(js[lo] == 2, b_ref, recv_b, slot, k)
        y_sends(js[lo] == 2, slot)
    y2 = wrap(y + 2, NY)
    slot = group(here, y2, 1)
    for k in (0, 1):
        arrived(home, b_ref, recv_b, slot, k)
    x_sends(home, slot)
    ring(2)
    for lo in (0, 1):
        for ys, k, to in ((ym, 0, to_yp), (yp, 1, to_ym)):
            slot = group(lo, ys, 0)
            arrived(None, b_ref, recv_b, slot)
            part(None, b_ref, recv_b, slot, k, to)
        x_pass(lo, group(lo, y, 1))
        for ys in (ym, yp):
            x_pass(lo, group(lo, ys, 1))
    ring(3)
    for lo in (0, 1):
        x_pass(lo, group(lo, y2, 1))
    for lo in (0, 1):
        for k in (0, 1):
            arrived(None, b_ref, recv_b, group(lo, y2, 0), k)
            for ys in (y, ym, yp, y2):
                arrived(js[lo] == 2, b_ref, recv_b, group(lo, ys, 1), k)
    slot = 2 * wrap(z + 4, NZ) + c
    for k in (0, 1):
        arrived(None, a_ref, recv_a, slot, k)
        part(None, a_ref, recv_a, slot, k, sib)
    for d in range(NZ):
        slot = 2 * wrap(z + d, NZ) + 1 - c
        if d == 4:
            for k in (0, 1):
                arrived(None, a_ref, recv_a, slot, k)
        else:
            arrived(None, a_ref, recv_a, slot)
    tails = [
        pltpu.make_async_copy(a_ref.at[:, tail], am_ref, local.at[0]),
        pltpu.make_async_copy(b_ref.at[:, tail], bm_ref, local.at[1]),
    ]
    for t in tails:
        t.start()
    for t in tails:
        t.wait()
    cp.finish()


def gather(x, meta):
    shape = jax.ShapeDtypeStruct((GROUPS, ROWS, 128), jnp.bfloat16)
    tails = jax.ShapeDtypeStruct((GROUPS, META, 128), jnp.bfloat16)
    return pl.pallas_call(
        gather_kernel,
        out_shape=(shape, shape, tails, tails),
        in_specs=[pl.BlockSpec(memory_space=pl.ANY)] * 2,
        out_specs=(pl.BlockSpec(memory_space=pl.ANY),) * 4,
        scratch_shapes=[
            pltpu.SemaphoreType.DMA((96,)),
            pltpu.SemaphoreType.DMA((GROUPS, 2)),
            pltpu.SemaphoreType.DMA((GROUPS, 2)),
            pltpu.SemaphoreType.DMA((4,)),
        ],
        compiler_params=pltpu.CompilerParams(collective_id=0, has_side_effects=True),
        name="gather_strip_and_panel",
    )(x, meta)


def product_kernel(slot_ref, a_ref, b_ref, o_ref, acc):
    i = pl.program_id(0)
    for q in range(LC):
        acc[q] = jnp.zeros_like(acc[q])

    @pl.loop(0, GROUPS)
    def _(t):
        code = slot_ref[i, t]

        @pl.when(code >= 0)
        def _():
            m = code // LC
            q = code - m * LC
            a_re, a_im = a_ref[t, :128, :], a_ref[t, 128:, :]
            row = pl.multiple_of(m * BLK, BLK)
            b = b_ref[t, pl.ds(row, BLK), :]
            b_re, b_im = b[:128], b[128:]
            lhs = jnp.concatenate([a_re, a_im], axis=1)
            rhs = jnp.concatenate(
                [jnp.concatenate([b_re, b_im], axis=1), jnp.concatenate([-b_im, b_re], axis=1)], axis=0
            )
            acc[q] += jnp.dot(lhs, rhs, preferred_element_type=jnp.float32)

    for q in range(LC):
        o_ref[0, q, 0] = acc[q][:, :128].astype(jnp.bfloat16)
        o_ref[0, q, 1] = acc[q][:, 128:].astype(jnp.bfloat16)


def product(code, a, b):
    return pl.pallas_call(
        product_kernel,
        out_shape=jax.ShapeDtypeStruct((RB, LC, 2, 128, 128), jnp.bfloat16),
        grid_spec=pltpu.PrefetchScalarGridSpec(
            num_scalar_prefetch=1,
            grid=(RB,),
            in_specs=[
                pl.BlockSpec((GROUPS, BLK, 128), lambda i, code: (0, i, 0)),
                pl.BlockSpec((GROUPS, ROWS, 128), lambda i, code: (0, 0, 0), pipeline_mode=pl.Buffered(1)),
            ],
            out_specs=pl.BlockSpec((1, LC, 2, 128, 128), lambda i, code: (i, 0, 0, 0, 0)),
            scratch_shapes=[pltpu.VMEM((LC, 128, 256), jnp.float32)],
        ),
        compiler_params=pltpu.CompilerParams(
            dimension_semantics=("arbitrary",), vmem_limit_bytes=32 << 20
        ),
        name="matched_block_products",
    )(code, a, b)


def swap_kernel(n, p_ref, o_ref, mid, send, recv_mid, recv, local):
    x, y, z, c = where_am_i()
    h = x // 2
    home = c == h
    away = c != h
    xp, xm = wrap(x + 1, NX), wrap(x - 1, NX)
    to = [device(xp, y, z, c), device(xm, y, z, c)]
    on = [device(xp, y, z, 1 - c), device(xm, y, z, 1 - c)]
    enter(to + on)
    cp = Copies(send)
    step = RB // (2 * n)
    keep = pltpu.make_async_copy(p_ref, o_ref, local.at[0])
    pl.when(home)(keep.start)

    def wait(cond, view, sem):
        pl.when(cond)(
            pltpu.make_async_remote_copy(
                src_ref=view, dst_ref=view, send_sem=send.at[0], recv_sem=sem, device_id=to[0], device_id_type=MESH
            ).wait_recv
        )

    def rows(ref, d, k):
        return ref.at[pl.ds((d * n + k) * step, step)]

    for k in range(n):
        for d in (0, 1):
            cp.start(away, rows(p_ref, d, k), rows(mid, d, k), recv_mid.at[d, k], to[d])
    from_away = [c != xm // 2, c != xp // 2]
    for k in range(n):
        for d in (0, 1):
            wait(from_away[d], rows(mid, d, k), recv_mid.at[d, k])
            cp.start(from_away[d], rows(mid, d, k), rows(o_ref, d, k), recv.at[d, k], on[d])
    for k in range(n):
        for d in (0, 1):
            wait(away, rows(o_ref, d, k), recv.at[d, k])
    pl.when(home)(keep.wait)
    cp.finish()


def swap_back(p):
    n = 3
    out, unused = pl.pallas_call(
        functools.partial(swap_kernel, n),
        out_shape=(jax.ShapeDtypeStruct(p.shape, p.dtype),) * 2,
        in_specs=[pl.BlockSpec(memory_space=pl.ANY)],
        out_specs=(pl.BlockSpec(memory_space=pl.ANY),) * 2,
        scratch_shapes=[
            pltpu.SemaphoreType.DMA((4 * n,)),
            pltpu.SemaphoreType.DMA((2, n)),
            pltpu.SemaphoreType.DMA((2, n)),
            pltpu.SemaphoreType.DMA((1,)),
        ],
        compiler_params=pltpu.CompilerParams(collective_id=1, has_side_effects=True),
        name="swap_results",
    )(p)
    return out


def on_device(x_blocks, x_cols, c_cols, c_keep):
    x = x_blocks.reshape(RB * BLK, 128)
    wanted = jnp.where(c_keep != 0, c_cols, -2)
    meta = jnp.concatenate([x_cols.T, wanted.T], axis=0)
    meta = jnp.pad(meta, ((0, META - 1 - LC), (0, 128 - RB))).astype(jnp.bfloat16)
    a, b, a_meta, b_meta = gather(x, meta)
    a_meta = a_meta[:, :, :RB].astype(jnp.int32)
    b_meta = b_meta[:, :, :RB].astype(jnp.int32)
    a_cols = a_meta[:, 0]
    pick = a_cols[:, :, None] == jnp.arange(RB)[None, None, :]
    column = jnp.sum(jnp.where(pick, b_meta[:, 0][:, None, :] + 1, 0), axis=2) - 1
    mine = lax.dynamic_index_in_dim(a_meta, lax.axis_index("section") // 2 * 2 + lax.rem(lax.axis_index("rows"), 2), 0, False)
    hit = (column[None] == mine[1 : 1 + LC][:, None, :]) & (column >= 0)[None]
    q = jnp.sum(jnp.where(hit, jnp.arange(1, LC + 1)[:, None, None], 0), axis=0)
    code = jnp.where(q > 0, a_cols * LC + q - 1, -1).T
    p = product(code, a, b)
    return swap_back(p)


def solution(mesh):
    spec = P("rows", "section")
    blocks = P("rows", "section", None, None, None)
    return jax.shard_map(
        on_device, mesh=mesh, in_specs=(blocks, spec, spec, spec), out_specs=blocks, check_vma=False
    )
```

time: 366 us -> 256 us (0.70)
  the two profiles are of different devices: /device:TPU:1 before, /device:TPU:2 now
where the time goes in v1:
time: 256 us
  Pallas kernels  241 us (94%)
  local copies, waits for them, and re-layouts  11 us (4%)
  other arithmetic  3.21 us (1%)
    pallas_call x1, Pallas kernels, gather(): pl.pallas_call(gather_kernel, out_shape=(shape, shape, tails, tails), in_...  142 us
    pallas_call x1, Pallas kernels, swap_back(): pl.pallas_call(functools.partial(swap_kernel, n), out_shape=(jax.ShapeDty...  82.1 us
    pallas_call x1, Pallas kernels, product(): pl.pallas_call(product_kernel, out_shape=jax.ShapeDtypeStruct((RB, LC, 2,...  17.6 us
    unnamed x5, local copies, waits for them, and re-layouts  9.36 us

profile of v1, /device:TPU:2, one launch (start us, length us, event | category | flops | bytes accessed | tf_op | source)
XLA Modules:
  0.0 255.6 jit_solution(9070434288859425503)
XLA Ops:
  0.0 0.7 convert_bitcast_fusion
  0.7 0.7 fusion.6
  1.4 0.6 fusion.5.m_ref
  2.0 141.7 %gather_strip_and_panel.1 = (bf16[16,3088,128]{2,1,0:T(8,128)(2,1)}, bf16[16,3088,128]{2,1,0:T(8,128)(2,1)}, bf16[16,16,128]{2,1,0:T(8,128)(2,1)}, bf16[16,16,128]{2,1,0:T(8,128)(2,1)}) custom-call(bf16[3072,128]{1,0:T(8,128)(2,1)} %bitcast.12, bf16[16,128]{1,0:T(8,128)(2,1)} %fusion.5.m_ref), custom_call_target="tpu_custom_call" | custom-call | tf_op jit(solution)/shard_map/gather_strip_and_panel/pallas_call | solution.py:253
  143.7 0.8 convert_add_fusion
  144.5 1.1 copy.13
  145.6 0.2 dynamic-slice_reduce_fusion
  145.8 0.4 select_reduce_fusion
  146.2 0.1 copy.14
  146.3 0.1 copy.15
  146.4 0.1 select_reduce_fusion.1
  146.5 0.1 copy.16
  146.6 0.0 copy-start
  146.6 4.6 %copy-done = bf16[16,3088,128]{2,1,0:T(8,128)(2,1)S(1)} copy-done((bf16[16,3088,128]{2,1,0:T(8,128)(2,1)S(1)}, bf16[16,3088,128]{2,1,0:T(8,128)(2,1)}, u32[]{:S(2)}) %copy-start) | copy-done | bytes 12648472
  151.2 17.6 %matched_block_products.1.p_ref = bf16[12,3,2,128,128]{4,3,2,1,0:T(8,128)(2,1)S(1)} custom-call(s32[12,16]{1,0:T(8,128)S(1)} %select_bitcast_fusion.slot_ref, bf16[16,3088,128]{2,1,0:T(8,128)(2,1)S(1)} %copy-done, bf16[16,3088,128]{2,1,0:T(8,128)(2,1)} %get-tuple-element.13.b_ref), custom_call_target="tpu_custom_call" | custom-call | tf_op jit(solution)/shard_map/matched_block_products/pallas_call | solution.py:298
  168.8 0.0 copy-start.1
  168.8 1.4 copy-done.1
  170.2 82.1 %swap_results.1 = (bf16[12,3,2,128,128]{4,3,2,1,0:T(8,128)(2,1)}, bf16[12,3,2,128,128]{4,3,2,1,0:T(8,128)(2,1)}) custom-call(bf16[12,3,2,128,128]{4,3,2,1,0:T(8,128)(2,1)} %copy-done.1), custom_call_target="tpu_custom_call" | custom-call | tf_op jit(solution)/shard_map/swap_results/pallas_call | solution.py:359
  252.3 3.4 %copy.19 = bf16[12,3,2,128,128]{4,3,2,1,0:T(8,128)(2,1)} copy(bf16[12,3,2,128,128]{4,3,2,1,0:T(8,128)(2,1)} %get-tuple-element.14) | data formatting | bytes 4718592
  (6 shorter events, 0.0 us)
Async XLA Ops:
  146.6 4.6 %copy-start = (bf16[16,3088,128]{2,1,0:T(8,128)(2,1)S(1)}, bf16[16,3088,128]{2,1,0:T(8,128)(2,1)}, u32[]{:S(2)}) copy-start(bf16[16,3088,128]{2,1,0:T(8,128)(2,1)} %get-tuple-element.12.a_ref) | copy-start | bytes 37945348
  168.8 1.4 copy-start.1

commit v2 on v1

--- a/solution.py
+++ b/solution.py
@@ -253,7 +253,7 @@
     return pl.pallas_call(
         gather_kernel,
         out_shape=(shape, shape, tails, tails),
-        in_specs=[pl.BlockSpec(memory_space=pl.ANY)] * 2,
+        in_specs=[pl.BlockSpec(memory_space=pltpu.VMEM)] * 2,
         out_specs=(pl.BlockSpec(memory_space=pl.ANY),) * 4,
         scratch_shapes=[
             pltpu.SemaphoreType.DMA((96,)),
@@ -315,62 +315,32 @@
     )(code, a, b)
 
 
-def swap_kernel(n, p_ref, o_ref, mid, send, recv_mid, recv, local):
+def swap_kernel(p_ref, o_ref, send, recv, local):
     x, y, z, c = where_am_i()
-    h = x // 2
-    home = c == h
-    away = c != h
-    xp, xm = wrap(x + 1, NX), wrap(x - 1, NX)
-    to = [device(xp, y, z, c), device(xm, y, z, c)]
-    on = [device(xp, y, z, 1 - c), device(xm, y, z, 1 - c)]
-    enter(to + on)
-    cp = Copies(send)
-    step = RB // (2 * n)
+    home = c == x // 2
+    away = c != x // 2
+    to = device(wrap(x + 2, NX), y, z, 1 - c)
+    enter([to])
     keep = pltpu.make_async_copy(p_ref, o_ref, local.at[0])
+    move = pltpu.make_async_remote_copy(
+        src_ref=p_ref, dst_ref=o_ref, send_sem=send, recv_sem=recv, device_id=to, device_id_type=MESH
+    )
     pl.when(home)(keep.start)
-
-    def wait(cond, view, sem):
-        pl.when(cond)(
-            pltpu.make_async_remote_copy(
-                src_ref=view, dst_ref=view, send_sem=send.at[0], recv_sem=sem, device_id=to[0], device_id_type=MESH
-            ).wait_recv
-        )
-
-    def rows(ref, d, k):
-        return ref.at[pl.ds((d * n + k) * step, step)]
-
-    for k in range(n):
-        for d in (0, 1):
-            cp.start(away, rows(p_ref, d, k), rows(mid, d, k), recv_mid.at[d, k], to[d])
-    from_away = [c != xm // 2, c != xp // 2]
-    for k in range(n):
-        for d in (0, 1):
-            wait(from_away[d], rows(mid, d, k), recv_mid.at[d, k])
-            cp.start(from_away[d], rows(mid, d, k), rows(o_ref, d, k), recv.at[d, k], on[d])
-    for k in range(n):
-        for d in (0, 1):
-            wait(away, rows(o_ref, d, k), recv.at[d, k])
+    pl.when(away)(move.start)
     pl.when(home)(keep.wait)
-    cp.finish()
+    pl.when(away)(move.wait)
 
 
 def swap_back(p):
-    n = 3
-    out, unused = pl.pallas_call(
-        functools.partial(swap_kernel, n),
-        out_shape=(jax.ShapeDtypeStruct(p.shape, p.dtype),) * 2,
-        in_specs=[pl.BlockSpec(memory_space=pl.ANY)],
-        out_specs=(pl.BlockSpec(memory_space=pl.ANY),) * 2,
-        scratch_shapes=[
-            pltpu.SemaphoreType.DMA((4 * n,)),
-            pltpu.SemaphoreType.DMA((2, n)),
-            pltpu.SemaphoreType.DMA((2, n)),
-            pltpu.SemaphoreType.DMA((1,)),
-        ],
+    return pl.pallas_call(
+        swap_kernel,
+        out_shape=jax.ShapeDtypeStruct(p.shape, p.dtype),
+        in_specs=[pl.BlockSpec(memory_space=pltpu.VMEM)],
+        out_specs=pl.BlockSpec(memory_space=pl.ANY),
+        scratch_shapes=[pltpu.SemaphoreType.DMA, pltpu.SemaphoreType.DMA, pltpu.SemaphoreType.DMA((1,))],
         compiler_params=pltpu.CompilerParams(collective_id=1, has_side_effects=True),
         name="swap_results",
     )(p)
-    return out
 
 
 def on_device(x_blocks, x_cols, c_cols, c_keep):

time: 256 us -> 163 us (0.64)
  the two profiles are of different devices: /device:TPU:2 before, /device:TPU:1 now
where the time goes in v2:
time: 163 us
  Pallas kernels  149 us (91%)
  local copies, waits for them, and re-layouts  11 us (7%)
  other arithmetic  3.21 us (2%)
    pallas_call x1, Pallas kernels, gather(): pl.pallas_call(gather_kernel, out_shape=(shape, shape, tails, tails), in_...  97.5 us
    pallas_call x1, Pallas kernels, swap_back(): pl.pallas_call(swap_kernel, out_shape=jax.ShapeDtypeStruct(p.shape, p.dty...  31.6 us
    pallas_call x1, Pallas kernels, product(): pl.pallas_call(product_kernel, out_shape=jax.ShapeDtypeStruct((RB, LC, 2,...  19.4 us
    unnamed x5, local copies, waits for them, and re-layouts  9.36 us

profile of v2, /device:TPU:1, one launch (start us, length us, event | category | flops | bytes accessed | tf_op | source)
XLA Modules:
  0.0 162.8 jit_solution(14119254938420644528)
XLA Ops:
  0.0 0.7 convert_bitcast_fusion
  0.7 0.7 fusion.6
  1.4 0.6 fusion.5.m_ref
  2.0 97.5 %gather_strip_and_panel.1 = (bf16[16,3088,128]{2,1,0:T(8,128)(2,1)}, bf16[16,3088,128]{2,1,0:T(8,128)(2,1)}, bf16[16,16,128]{2,1,0:T(8,128)(2,1)}, bf16[16,16,128]{2,1,0:T(8,128)(2,1)}) custom-call(bf16[3072,128]{1,0:T(8,128)(2,1)} %bitcast.12, bf16[16,128]{1,0:T(8,128)(2,1)} %fusion.5.m_ref), custom_call_target="tpu_custom_call" | custom-call | tf_op jit(solution)/shard_map/gather_strip_and_panel/pallas_call | solution.py:253
  99.5 0.8 convert_add_fusion
  100.3 1.1 copy.13
  101.4 0.2 dynamic-slice_reduce_fusion
  101.6 0.4 select_reduce_fusion
  102.0 0.1 copy.14
  102.1 0.1 copy.15
  102.2 0.1 select_reduce_fusion.1
  102.3 0.1 copy.16
  102.4 0.0 copy-start
  102.4 4.6 %copy-done = bf16[16,3088,128]{2,1,0:T(8,128)(2,1)S(1)} copy-done((bf16[16,3088,128]{2,1,0:T(8,128)(2,1)S(1)}, bf16[16,3088,128]{2,1,0:T(8,128)(2,1)}, u32[]{:S(2)}) %copy-start) | copy-done | bytes 12648472
  107.0 19.4 %matched_block_products.1.p_ref = bf16[12,3,2,128,128]{4,3,2,1,0:T(8,128)(2,1)S(1)} custom-call(s32[12,16]{1,0:T(8,128)S(1)} %select_bitcast_fusion.slot_ref, bf16[16,3088,128]{2,1,0:T(8,128)(2,1)S(1)} %copy-done, bf16[16,3088,128]{2,1,0:T(8,128)(2,1)} %get-tuple-element.12.b_ref), custom_call_target="tpu_custom_call" | custom-call | tf_op jit(solution)/shard_map/matched_block_products/pallas_call | solution.py:298
  126.4 0.0 copy-start.1
  126.4 1.4 copy-done.1
  127.8 31.6 %swap_results.1 = bf16[12,3,2,128,128]{4,3,2,1,0:T(8,128)(2,1)} custom-call(bf16[12,3,2,128,128]{4,3,2,1,0:T(8,128)(2,1)} %copy-done.1), custom_call_target="tpu_custom_call" | custom-call | tf_op jit(solution)/shard_map/swap_results/pallas_call | solution.py:335
  159.4 3.4 %copy.19 = bf16[12,3,2,128,128]{4,3,2,1,0:T(8,128)(2,1)} copy(bf16[12,3,2,128,128]{4,3,2,1,0:T(8,128)(2,1)} %swap_results.1) | data formatting | bytes 4718592
  (6 shorter events, 0.0 us)
Async XLA Ops:
  102.4 4.6 %copy-start = (bf16[16,3088,128]{2,1,0:T(8,128)(2,1)S(1)}, bf16[16,3088,128]{2,1,0:T(8,128)(2,1)}, u32[]{:S(2)}) copy-start(bf16[16,3088,128]{2,1,0:T(8,128)(2,1)} %get-tuple-element.11.a_ref) | copy-start | bytes 37945348
  126.4 1.4 copy-start.1

commit v3 on v2

v3 whole, which is shorter than its diff:
```python
import jax
import jax.numpy as jnp
from jax import lax
from jax.experimental import pallas as pl
from jax.experimental.pallas import tpu as pltpu
from jax.sharding import PartitionSpec as P

MESH = pl.DeviceIdType.MESH
NX, NY, NZ, NC = 4, 4, 8, 2
RB = 12
GROUPS = 16
BLK = 256
HALF = RB // 2
META = 8
LC = 3
SLOTS = 16


def where_am_i():
    r, s = lax.axis_index("rows"), lax.axis_index("section")
    c = lax.rem(r, 2)
    y = lax.rem(r // 2, NY)
    x = lax.rem(s, 2) * 2 + r // 8
    return x, y, s // 2, c


def device(x, y, z, c):
    return ((lax.rem(x, 2) * NY + y) * 2 + c, z * 2 + x // 2)


def wrap(v, n):
    return lax.rem(v + n, n)


class Copies:
    def __init__(self, send):
        self.send, self.used, self.pending = send, 0, []

    def start(self, cond, src, dst, recv, to):
        copy = pltpu.make_async_remote_copy(
            src_ref=src, dst_ref=dst, send_sem=self.send.at[self.used], recv_sem=recv,
            device_id=to, device_id_type=MESH,
        )
        self.used += 1
        if cond is None:
            copy.start()
        else:
            pl.when(cond)(copy.start)
        self.pending.append((cond, copy))

    def finish(self):
        for cond, copy in self.pending:
            if cond is None:
                copy.wait_send()
            else:
                pl.when(cond)(copy.wait_send)


def enter(partners):
    barrier = pltpu.get_barrier_semaphore()
    for to in partners:
        pl.semaphore_signal(barrier, inc=1, device_id=to, device_id_type=MESH)
    pl.semaphore_wait(barrier, len(partners))


def square_kernel(
    x_ref, m_ref, o_ref, a_ref, b_ref, am_ref, bm_ref, c_ref, tab_v, tab_s,
    send, recv_a, recv_b, recv_m, send_c, recv_c, local,
):
    x, y, z, c = where_am_i()
    h = x // 2
    home = c == h
    away = c != h
    xp, xm = wrap(x + 1, NX), wrap(x - 1, NX)
    yp, ym = wrap(y + 1, NY), wrap(y - 1, NY)
    zp, zm = wrap(z + 1, NZ), wrap(z - 1, NZ)
    sib = device(x, y, z, 1 - c)
    swap = device(wrap(x + 2, NX), y, z, 1 - c)
    to_xp, to_xm = device(xp, y, z, c), device(xm, y, z, c)
    to_yp, to_ym = device(x, yp, z, c), device(x, ym, z, c)
    to_zp, to_zm = device(x, y, zp, c), device(x, y, zm, c)
    enter([sib, swap, to_xp, to_xm, to_yp, to_ym, to_zp, to_zm])
    cp = Copies(send)
    strip = (a_ref, am_ref, recv_a, 0)
    panel = (b_ref, bm_ref, recv_b, 1)

    def half(ref, slot, k):
        return ref.at[slot, pl.ds(k * HALF, HALF)]

    def wait_for(cond, view, sem):
        wait = pltpu.make_async_remote_copy(
            src_ref=view, dst_ref=view, send_sem=send.at[0], recv_sem=sem, device_id=sib, device_id_type=MESH
        ).wait_recv
        if cond is None:
            wait()
        else:
            pl.when(cond)(wait)

    def arrived(cond, kind, slot, part=None):
        ref, meta, recv, k = kind
        view = ref.at[slot] if part is None else half(ref, slot, part)
        wait_for(cond, view, recv.at[slot, part or 0])
        if part != 1:
            wait_for(cond, meta.at[slot], recv_m.at[k, slot])

    def full(cond, kind, slot, to):
        ref, meta, recv, k = kind
        cp.start(cond, meta.at[slot], meta.at[slot], recv_m.at[k, slot], to)
        cp.start(cond, ref.at[slot], ref.at[slot], recv.at[slot, 0], to)

    def part(cond, kind, slot, p, to):
        ref, meta, recv, k = kind
        if p == 0:
            cp.start(cond, meta.at[slot], meta.at[slot], recv_m.at[k, slot], to)
        cp.start(cond, half(ref, slot, p), half(ref, slot, p), recv.at[slot, p], to)

    def group(lo, ys, core):
        return (lo * NY + ys) * 2 + core

    here = lax.rem(x, 2)
    own = group(here, y, c)
    a_own = 2 * z + c
    a_partner = 2 * z + (1 - c)

    def give(kind, slot, to):
        ref, meta, recv, k = kind
        cp.start(away, m_ref, meta.at[slot], recv_m.at[k, slot], to)
        cp.start(away, x_ref, ref.at[slot], recv.at[slot, 0], to)

    give(strip, a_partner, swap)
    give(panel, own, sib)

    def keep(kind, slot):
        ref, meta, recv, k = kind
        ref[slot] = x_ref[...]
        meta[slot] = m_ref[...]

    @pl.when(home)
    def _():
        keep(strip, a_own)
        keep(panel, own)

    def z_own(cond):
        for to in (to_zp, to_zm, sib):
            full(cond, strip, a_own, to)

    z_own(home)
    arrived(home, panel, group(here, y, 1 - c))
    mine_x, mine_y = group(here, y, 0), group(here, y, 1)
    for to in (to_xp, to_xm):
        full(home, panel, mine_x, to)
    for to in (to_yp, to_ym):
        full(home, panel, mine_y, to)
    for to in (to_yp, to_ym):
        full(home, panel, mine_x, to)
    for to in (to_xp, to_xm):
        full(home, panel, mine_y, to)
    arrived(away, strip, a_own)
    z_own(away)

    js = [wrap(x - 2 * c - lo, NX) for lo in (0, 1)]

    def y_sends(cond, slot):
        full(cond, panel, slot, to_yp)
        full(cond, panel, slot, to_ym)

    def x_sends(cond, slot):
        full(cond, panel, slot, to_xp)
        full(cond, panel, slot, to_xm)

    def ring(d):
        for zs, k, to in ((wrap(z - d, NZ), 0, to_zp), (wrap(z + d, NZ), 1, to_zm)):
            slot = 2 * zs + c
            arrived(None, strip, slot)
            if d < 3:
                full(None, strip, slot, to)
            else:
                part(None, strip, slot, k, to)
            full(None, strip, slot, sib)

    def x_pass(lo, slot):
        j = js[lo]
        for jj, k, to in ((1, 0, to_xp), (3, 1, to_xm)):
            arrived(j == jj, panel, slot)
            part(j == jj, panel, slot, k, to)

    for lo in (0, 1):
        slot = group(lo, y, 0)
        x_pass(lo, slot)
        y_sends((js[lo] == 1) | (js[lo] == 3), slot)
    for ys, k, to in ((ym, 0, to_yp), (yp, 1, to_ym)):
        slot = group(here, ys, 1)
        arrived(home, panel, slot)
        part(home, panel, slot, k, to)
        x_sends(home, slot)
    ring(1)
    for lo in (0, 1):
        slot = group(lo, y, 0)
        for k in (0, 1):
            arrived(js[lo] == 2, panel, slot, k)
        y_sends(js[lo] == 2, slot)
    y2 = wrap(y + 2, NY)
    slot = group(here, y2, 1)
    for k in (0, 1):
        arrived(home, panel, slot, k)
    x_sends(home, slot)
    ring(2)
    for lo in (0, 1):
        for ys, k, to in ((ym, 0, to_yp), (yp, 1, to_ym)):
            slot = group(lo, ys, 0)
            arrived(None, panel, slot)
            part(None, panel, slot, k, to)
        x_pass(lo, group(lo, y, 1))
        for ys in (ym, yp):
            x_pass(lo, group(lo, ys, 1))
    ring(3)
    for lo in (0, 1):
        x_pass(lo, group(lo, y2, 1))
    for lo in (0, 1):
        for k in (0, 1):
            arrived(None, panel, group(lo, y2, 0), k)
            for ys in (y, ym, yp, y2):
                arrived(js[lo] == 2, panel, group(lo, ys, 1), k)
    slot = 2 * wrap(z + 4, NZ) + c
    for k in (0, 1):
        arrived(None, strip, slot, k)
        part(None, strip, slot, k, sib)
    for d in range(NZ):
        slot = 2 * wrap(z + d, NZ) + 1 - c
        if d == 4:
            for k in (0, 1):
                arrived(None, strip, slot, k)
        else:
            arrived(None, strip, slot)

    sub = lax.broadcasted_iota(jnp.int32, (SLOTS, 128), 0)
    lane = lax.broadcasted_iota(jnp.int32, (SLOTS, 128), 1)

    def upright(row):
        return jnp.sum(jnp.where(lane == sub, row, 0), axis=1, keepdims=True)

    wanted = [upright(am_ref[a_own, pl.ds(1 + q, 1), :]) for q in range(LC)]
    blocks = codes = jnp.zeros((SLOTS, 128), jnp.int32)
    for t in range(GROUPS):
        col = upright(am_ref[t, pl.ds(0, 1), :])
        far = jnp.sum(jnp.where(lane == col, bm_ref[t, pl.ds(0, 1), :] + 1, 0), axis=1, keepdims=True) - 1
        code = jnp.zeros_like(col)
        for q in range(LC):
            code = code + jnp.where((col >= 0) & (far >= 0) & (far == wanted[q]), q + 1, 0)
        blocks = jnp.where(lane == t, jnp.maximum(col, 0), blocks)
        codes = jnp.where(lane == t, code, codes)
    tab_v[0] = blocks
    tab_v[1] = codes
    to_smem = pltpu.make_async_copy(tab_v.at[0], tab_s, local.at[0])
    to_smem.start()
    to_smem.wait()

    def moved(i):
        return pltpu.make_async_remote_copy(
            src_ref=c_ref.at[i], dst_ref=o_ref.at[i], send_sem=send_c.at[i], recv_sem=recv_c.at[i],
            device_id=swap, device_id_type=MESH,
        )

    def stored(i):
        return pltpu.make_async_copy(c_ref.at[i], o_ref.at[i], send_c.at[i])

    @pl.loop(0, RB)
    def _(i):
        row_codes = tab_v[1, pl.ds(i, 1), :]
        masks = [jnp.where(row_codes == k + 1, 1.0, 0.0).astype(jnp.bfloat16) for k in range(LC)]
        total = None
        for t in range(GROUPS):
            a = a_ref[t, i]
            lhs = jnp.concatenate([a[:128], a[128:]], axis=1)
            lhs = jnp.concatenate([lhs * masks[k][:, t : t + 1] for k in range(LC)], axis=0)
            b = b_ref[t, tab_s[i, t]]
            rhs = jnp.concatenate(
                [jnp.concatenate([b[:128], b[128:]], axis=1), jnp.concatenate([-b[128:], b[:128]], axis=1)], axis=0
            )
            term = jnp.dot(lhs, rhs, preferred_element_type=jnp.float32)
            total = term if total is None else total + term
        for k in range(LC):
            for part_of in (0, 1):
                c_ref[i, k, part_of] = total[128 * k : 128 * (k + 1), 128 * part_of : 128 * (part_of + 1)].astype(
                    jnp.bfloat16
                )

        @pl.when(away)
        def _():
            moved(i).start()

        @pl.when(home)
        def _():
            stored(i).start()

    @pl.loop(0, RB)
    def _(i):
        @pl.when(away)
        def _():
            moved(i).wait()

        @pl.when(home)
        def _():
            stored(i).wait()

    cp.finish()


def square(x, meta):
    dma = pltpu.SemaphoreType.DMA
    return pl.pallas_call(
        square_kernel,
        out_shape=jax.ShapeDtypeStruct((RB, LC, 2, 128, 128), jnp.bfloat16),
        in_specs=[pl.BlockSpec(memory_space=pltpu.VMEM)] * 2,
        out_specs=pl.BlockSpec(memory_space=pl.ANY),
        scratch_shapes=[
            pltpu.VMEM((GROUPS, RB, BLK, 128), jnp.bfloat16),
            pltpu.VMEM((GROUPS, RB, BLK, 128), jnp.bfloat16),
            pltpu.VMEM((GROUPS, META, 128), jnp.int32),
            pltpu.VMEM((GROUPS, META, 128), jnp.int32),
            pltpu.VMEM((RB, LC, 2, 128, 128), jnp.bfloat16),
            pltpu.VMEM((2, SLOTS, 128), jnp.int32),
            pltpu.SMEM((SLOTS, 128), jnp.int32),
            dma((128,)),
            dma((GROUPS, 2)),
            dma((GROUPS, 2)),
            dma((2, GROUPS)),
            dma((RB,)),
            dma((RB,)),
            dma((1,)),
        ],
        compiler_params=pltpu.CompilerParams(
            collective_id=0, has_side_effects=True, vmem_limit_bytes=48 << 20
        ),
        name="gather_and_square",
    )(x, meta)


def on_device(x_blocks, x_cols, c_cols, c_keep):
    x = x_blocks.reshape(RB, BLK, 128)
    wanted = jnp.where(c_keep != 0, c_cols, -2)
    meta = jnp.concatenate([x_cols.T, wanted.T], axis=0)
    meta = jnp.pad(meta, ((0, META - 1 - LC), (0, 128 - RB)), constant_values=-1)
    return square(x, meta)


def solution(mesh):
    spec = P("rows", "section")
    blocks = P("rows", "section", None, None, None)
    return jax.shard_map(
        on_device, mesh=mesh, in_specs=(blocks, spec, spec, spec), out_specs=blocks, check_vma=False
    )
```

time: 163 us -> 123 us (0.75)
  Pallas kernels: 149 us -> 119 us
  local copies, waits for them, and re-layouts: 11 us -> 2.54 us
  other arithmetic: 3.21 us -> 1.36 us
    pallas_call x3 -> x1, Pallas kernels: 149 us -> 119 us  [square(): pl.pallas_call(square_kernel, out_shape=jax.ShapeDtypeStruct((RB, LC, 2,...]
    unnamed x5 -> x3, local copies, waits for them, and re-layouts: 9.36 us -> 2.53 us
where the time goes in v3:
time: 123 us
  Pallas kernels  119 us (97%)
  local copies, waits for them, and re-layouts  2.54 us (2%)
  other arithmetic  1.36 us (1%)
    pallas_call x1, Pallas kernels, square(): pl.pallas_call(square_kernel, out_shape=jax.ShapeDtypeStruct((RB, LC, 2,...  119 us
    unnamed x3, local copies, waits for them, and re-layouts  2.53 us

profile of v3, /device:TPU:1, one launch (start us, length us, event | category | flops | bytes accessed | tf_op | source)
XLA Modules:
  0.0 122.7 jit_solution(14709058316563754861)
XLA Ops:
  0.0 0.7 select_bitcast_fusion
  0.7 0.7 pad_add_fusion
  1.4 0.0 copy-start
  1.4 1.1 copy-done
  2.5 118.8 %gather_and_square.1 = bf16[12,3,2,128,128]{4,3,2,1,0:T(8,128)(2,1)S(1)} custom-call(bf16[12,256,128]{2,1,0:T(8,128)(2,1)S(1)} %bitcast.4, s32[8,128]{1,0:T(8,128)S(1)} %pad.4.m_ref), custom_call_target="tpu_custom_call" | custom-call | tf_op jit(solution)/shard_map/gather_and_square/pallas_call | solution.py:311
  121.3 1.4 %copy.6 = bf16[12,3,2,128,128]{4,3,2,1,0:T(8,128)(2,1)} copy(bf16[12,3,2,128,128]{4,3,2,1,0:T(8,128)(2,1)S(1)} %gather_and_square.1) | data formatting | bytes 4718592
  (1 shorter events, 0.0 us)
Async XLA Ops:
  1.4 1.1 copy-start

commit v4 on v3

v4 whole, which is shorter than its diff:
```python
import jax
import jax.numpy as jnp
from jax import lax
from jax.experimental import pallas as pl
from jax.experimental.pallas import tpu as pltpu
from jax.sharding import PartitionSpec as P

MESH = pl.DeviceIdType.MESH
NX, NY, NZ, NC = 4, 4, 8, 2
RB = 12
GROUPS = 16
BLK = 256
HALF = RB // 2
META = 8
LC = 3
SLOTS = 16
SENDS = 194


def where_am_i():
    r, s = lax.axis_index("rows"), lax.axis_index("section")
    c = lax.rem(r, 2)
    y = lax.rem(r // 2, NY)
    x = lax.rem(s, 2) * 2 + r // 8
    return x, y, s // 2, c


def device(x, y, z, c):
    return ((lax.rem(x, 2) * NY + y) * 2 + c, z * 2 + x // 2)


def wrap(v, n):
    return lax.rem(v + n, n)


class Copies:
    def __init__(self, send):
        self.send, self.used, self.pending = send, 0, []

    def start(self, cond, src, dst, recv, to):
        copy = pltpu.make_async_remote_copy(
            src_ref=src, dst_ref=dst, send_sem=self.send.at[self.used], recv_sem=recv,
            device_id=to, device_id_type=MESH,
        )
        self.used += 1
        if cond is None:
            copy.start()
        else:
            pl.when(cond)(copy.start)
        self.pending.append((cond, copy))

    def finish(self):
        for cond, copy in self.pending:
            if cond is None:
                copy.wait_send()
            else:
                pl.when(cond)(copy.wait_send)


def enter(partners):
    barrier = pltpu.get_barrier_semaphore()
    for to in partners:
        pl.semaphore_signal(barrier, inc=1, device_id=to, device_id_type=MESH)
    pl.semaphore_wait(barrier, len(partners))


def square_kernel(
    x_ref, xc_ref, cc_ref, ck_ref, o_ref, a_ref, b_ref, am_ref, bm_ref, m_ref, c_ref, tab_v, tab_s,
    send, recv_a, recv_b, recv_m, send_c, recv_c, local,
):
    x, y, z, c = where_am_i()
    h = x // 2
    home = c == h
    away = c != h
    xp, xm = wrap(x + 1, NX), wrap(x - 1, NX)
    yp, ym, y2 = wrap(y + 1, NY), wrap(y - 1, NY), wrap(y + 2, NY)
    zp, zm = wrap(z + 1, NZ), wrap(z - 1, NZ)
    sib = device(x, y, z, 1 - c)
    swap = device(wrap(x + 2, NX), y, z, 1 - c)
    to_xp, to_xm = device(xp, y, z, c), device(xm, y, z, c)
    to_yp, to_ym = device(x, yp, z, c), device(x, ym, z, c)
    to_zp, to_zm = device(x, y, zp, c), device(x, y, zm, c)
    here = lax.rem(x, 2)

    def group(lo, ys, core):
        return (lo * NY + ys) * 2 + core

    own = group(here, y, c)
    a_own = 2 * z + c
    a_partner = 2 * z + (1 - c)

    mine = [
        pltpu.make_async_copy(x_ref, a_ref.at[a_own], local.at[0]),
        pltpu.make_async_copy(x_ref, b_ref.at[own], local.at[1]),
    ]

    @pl.when(home)
    def _():
        for copy in mine:
            copy.start()

    m_ref[...] = jnp.full((META, 128), -1, jnp.int32)
    m_ref[0:1, 0:RB] = xc_ref[...]
    m_ref[1 : 1 + LC, 0:RB] = jnp.where(ck_ref[...] != 0, cc_ref[...], -2)

    @pl.when(home)
    def _():
        am_ref[a_own] = m_ref[...]
        bm_ref[own] = m_ref[...]

    enter([sib, swap, device(wrap(x + 2, NX), y, z, c), to_xp, to_xm, to_yp, to_ym, to_zp, to_zm])
    cp = Copies(send)

    def wait_for(cond, view, sem):
        wait = pltpu.make_async_remote_copy(
            src_ref=view, dst_ref=view, send_sem=send.at[0], recv_sem=sem, device_id=sib, device_id_type=MESH
        ).wait_recv
        if cond is None:
            wait()
        else:
            pl.when(cond)(wait)

    def a_view(slot, core, k):
        rows = HALF if k is None else HALF // 2
        return a_ref.at[slot, pl.ds(core * HALF + (k or 0) * rows, rows)]

    def a_send(cond, slot, to, k=None):
        if k != 1:
            cp.start(cond, am_ref.at[slot], am_ref.at[slot], recv_m.at[0, slot], to)
        cp.start(cond, a_view(slot, c, k), a_view(slot, c, k), recv_a.at[slot, k or 0], to)

    def a_sib(cond, slot, k=None):
        cp.start(cond, a_view(slot, c, k), a_view(slot, c, k), recv_a.at[slot, 2 + (k or 0)], sib)

    def a_wait(cond, slot, k=None):
        wait_for(cond, a_view(slot, c, k), recv_a.at[slot, k or 0])
        if k != 1:
            wait_for(cond, am_ref.at[slot], recv_m.at[0, slot])

    def a_wait_sib(cond, slot, k=None):
        wait_for(cond, a_view(slot, 1 - c, k), recv_a.at[slot, 2 + (k or 0)])

    def b_view(slot, unit, k):
        _, first, rows, _ = unit
        if k is not None:
            rows = rows // 2
            first = first + k * rows
        return b_ref.at[slot, pl.ds(first, rows)]

    def b_send(cond, slot, unit, to, k=None):
        if k != 1 and unit[3] == 0:
            cp.start(cond, bm_ref.at[slot], bm_ref.at[slot], recv_m.at[1, slot], to)
        cp.start(cond, b_view(slot, unit, k), b_view(slot, unit, k), recv_b.at[slot, unit[3], k or 0], to)

    def b_wait(cond, slot, unit, k=None):
        wait_for(cond, b_view(slot, unit, k), recv_b.at[slot, unit[3], k or 0])
        if k != 1 and unit[3] == 0:
            wait_for(cond, bm_ref.at[slot], recv_m.at[1, slot])

    x_first = [(0, 0, RB, 0), (1, 0, 2, 0)]
    y_first = (1, 2, RB - 2, 1)

    for core in (0, 1):
        to = device(wrap(x + 2, NX), y, z, core)
        cp.start(away, m_ref, am_ref.at[a_partner], recv_m.at[0, a_partner], to)
        cp.start(away, x_ref.at[pl.ds(core * HALF, HALF)], a_view(a_partner, core, None), recv_a.at[a_partner, 0], to)
    cp.start(away, m_ref, bm_ref.at[own], recv_m.at[1, own], sib)
    cp.start(away, x_ref, b_ref.at[own], recv_b.at[own, 0, 0], sib)

    @pl.when(home)
    def _():
        for copy in mine:
            copy.wait()

    def z_own(cond, slot):
        for to in (to_zp, to_zm):
            a_send(cond, slot, to)

    a_first, a_swapped = 2 * z + h, 2 * z + 1 - h
    cp.start(home, am_ref.at[a_first], am_ref.at[a_first], recv_m.at[0, a_first], sib)
    cp.start(home, a_view(a_first, 1 - c, None), a_view(a_first, 1 - c, None), recv_a.at[a_first, 0], sib)
    z_own(home, a_first)
    a_sib(home, a_first)
    a_wait(away, a_first)
    z_own(away, a_first)
    from_sib = group(here, y, 1 - c)
    wait_for(home, b_ref.at[from_sib], recv_b.at[from_sib, 0, 0])
    wait_for(home, bm_ref.at[from_sib], recv_m.at[1, from_sib])

    def x_sends(cond, slot, unit):
        for to in (to_xp, to_xm):
            b_send(cond, slot, unit, to)

    def y_sends(cond, slot, unit):
        for to in (to_yp, to_ym):
            b_send(cond, slot, unit, to)

    js = [wrap(x - 2 * c - lo, NX) for lo in (0, 1)]
    beside = [(j == 1) | (j == 3) for j in js]

    def x_pass(cond, lo, ys, unit):
        slot = group(lo, ys, unit[0])
        for jj, k, to in ((1, 0, to_xp), (3, 1, to_xm)):
            on = cond & (js[lo] == jj)
            b_wait(on, slot, unit)
            b_send(on, slot, unit, to, k)

    def x_end(lo, ys, unit):
        for k in (0, 1):
            b_wait(js[lo] == 2, group(lo, ys, unit[0]), unit, k)

    def y_pass(cond, lo, unit):
        for ys, k, to in ((ym, 0, to_yp), (yp, 1, to_ym)):
            slot = group(lo, ys, unit[0])
            b_wait(cond, slot, unit)
            b_send(cond, slot, unit, to, k)

    def y_end(cond, lo, unit):
        for k in (0, 1):
            b_wait(cond, group(lo, y2, unit[0]), unit, k)

    def ring(d):
        for par in (h, 1 - h):
            for zs, k, to in ((wrap(z - d, NZ), 0, to_zp), (wrap(z + d, NZ), 1, to_zm)):
                slot = 2 * zs + par
                a_wait(None, slot)
                a_send(None, slot, to, k if d == 3 else None)
                a_sib(None, slot)

    x_sends(home, group(here, y, 0), x_first[0])
    y_sends(home, group(here, y, 1), y_first)
    x_sends(home, group(here, y, 1), x_first[1])
    y_sends(home, group(here, y, 0), x_first[0])
    y_sends(home, group(here, y, 1), x_first[1])
    x_sends(home, group(here, y, 1), y_first)

    a_wait(None, a_swapped)
    z_own(None, a_swapped)
    a_sib(None, a_swapped)
    for lo in (0, 1):
        x_pass(True, lo, y, x_first[0])
        y_sends(away & beside[lo], group(lo, y, 0), x_first[0])
    for lo in (0, 1):
        x_pass(True, lo, y, x_first[1])
        y_sends(away & beside[lo], group(lo, y, 1), x_first[1])
    y_pass(home, here, y_first)
    for ys in (ym, yp):
        x_sends(home, group(here, ys, 1), y_first)
    ring(1)
    for lo in (0, 1):
        x_end(lo, y, x_first[0])
        y_sends(js[lo] == 2, group(lo, y, 0), x_first[0])
    for lo in (0, 1):
        x_end(lo, y, x_first[1])
        y_sends(js[lo] == 2, group(lo, y, 1), x_first[1])
    y_end(home, here, y_first)
    x_sends(home, group(here, y2, 1), y_first)
    ring(2)
    for lo in (0, 1):
        y_pass(away, lo, x_first[0])
    for lo in (0, 1):
        y_pass(away, lo, x_first[1])
    for unit in x_first:
        y_pass(home, here, unit)
    for lo in (0, 1):
        x_pass(True, lo, y, y_first)
    for unit in x_first:
        for lo in (0, 1):
            y_sends(home & beside[lo], group(lo, y, unit[0]), unit)
    for lo in (0, 1):
        x_pass(True, lo, ym, y_first)
    for lo in (0, 1):
        x_pass(True, lo, yp, y_first)
    ring(3)
    for lo in (0, 1):
        x_pass(True, lo, y2, y_first)
    for unit in x_first:
        for lo in (0, 1):
            y_end(away, lo, unit)
    for ys in (y, ym, yp, y2):
        for lo in (0, 1):
            x_end(lo, ys, y_first)
    for unit in x_first:
        for lo in (0, 1):
            y_pass(home & beside[lo], lo, unit)

    for par in (h, 1 - h):
        slot = 2 * wrap(z + 4, NZ) + par
        for k in (0, 1):
            a_wait(None, slot, k)
            a_sib(None, slot, k)
    a_wait_sib(away, a_first)
    a_wait_sib(None, a_swapped)
    for d in range(1, NZ):
        for par in (h, 1 - h):
            for k in (0, 1) if d == 4 else (None,):
                a_wait_sib(None, 2 * wrap(z + d, NZ) + par, k)

    for unit in x_first:
        for lo in (0, 1):
            y_end(home, lo, unit)

    order = [group(lo, ys, core) for ys in (y, ym, yp, y2) for lo in (0, 1) for core in (0, 1)]
    sub = lax.broadcasted_iota(jnp.int32, (SLOTS, 128), 0)
    lane = lax.broadcasted_iota(jnp.int32, (SLOTS, 128), 1)

    def upright(row):
        return jnp.sum(jnp.where(lane == sub, row, 0), axis=1, keepdims=True)

    def look_up(places):
        wanted = [upright(am_ref[a_own, pl.ds(1 + q, 1), :]) for q in range(LC)]
        blocks = codes = jnp.zeros((SLOTS, 128), jnp.int32)
        for p in places:
            t = order[p]
            col = upright(am_ref[t, pl.ds(0, 1), :])
            far = jnp.sum(jnp.where(lane == col, bm_ref[t, pl.ds(0, 1), :] + 1, 0), axis=1, keepdims=True) - 1
            code = jnp.zeros_like(col)
            for q in range(LC):
                code = code + jnp.where((col >= 0) & (far >= 0) & (far == wanted[q]), q + 1, 0)
            blocks = jnp.where(lane == p, jnp.maximum(col, 0), blocks)
            codes = jnp.where(lane == p, code, codes)
        tab_v[0] = blocks
        tab_v[1] = codes
        to_smem = pltpu.make_async_copy(tab_v.at[0], tab_s, local.at[2])
        to_smem.start()
        to_smem.wait()

    def multiply(i, places, total):
        row_codes = tab_v[1, pl.ds(i, 1), :]
        masks = [jnp.where(row_codes == k + 1, 1.0, 0.0).astype(jnp.bfloat16) for k in range(LC)]
        for p in places:
            t = order[p]
            a = a_ref[t, i]
            lhs = jnp.concatenate([a[:128], a[128:]], axis=1)
            lhs = jnp.concatenate([lhs * masks[k][:, p : p + 1] for k in range(LC)], axis=0)
            b = b_ref[t, tab_s[i, p]]
            rhs = jnp.concatenate(
                [jnp.concatenate([b[:128], b[128:]], axis=1), jnp.concatenate([-b[128:], b[:128]], axis=1)], axis=0
            )
            term = jnp.dot(lhs, rhs, preferred_element_type=jnp.float32)
            total = term if total is None else total + term
        return total

    def finish_row(i, total):
        for k in range(LC):
            for p in (0, 1):
                c_ref[i, k, p] = total[128 * k : 128 * (k + 1), 128 * p : 128 * (p + 1)].astype(jnp.bfloat16)

    def moved(i):
        return pltpu.make_async_remote_copy(
            src_ref=c_ref.at[i], dst_ref=o_ref.at[i], send_sem=send_c.at[i], recv_sem=recv_c.at[i],
            device_id=swap, device_id_type=MESH,
        )

    def stored(i):
        return pltpu.make_async_copy(c_ref.at[i], o_ref.at[i], send_c.at[i])

    look_up(range(GROUPS))

    @pl.loop(0, RB)
    def _(i):
        finish_row(i, multiply(i, range(GROUPS), None))

        @pl.when(away)
        def _():
            moved(i).start()

        @pl.when(home)
        def _():
            stored(i).start()

    @pl.loop(0, RB)
    def _(i):
        @pl.when(away)
        def _():
            moved(i).wait()

        @pl.when(home)
        def _():
            stored(i).wait()

    cp.finish()


def square(x, x_cols, c_cols, c_keep):
    dma = pltpu.SemaphoreType.DMA
    vmem = pltpu.VMEM
    return pl.pallas_call(
        square_kernel,
        out_shape=jax.ShapeDtypeStruct((RB, LC, 2, 128, 128), jnp.bfloat16),
        in_specs=[pl.BlockSpec(memory_space=pltpu.HBM)] + [pl.BlockSpec(memory_space=vmem)] * 3,
        out_specs=pl.BlockSpec(memory_space=pl.ANY),
        scratch_shapes=[
            vmem((GROUPS, RB, BLK, 128), jnp.bfloat16),
            vmem((GROUPS, RB, BLK, 128), jnp.bfloat16),
            vmem((GROUPS, META, 128), jnp.int32),
            vmem((GROUPS, META, 128), jnp.int32),
            vmem((META, 128), jnp.int32),
            vmem((RB, LC, 2, 128, 128), jnp.bfloat16),
            vmem((2, SLOTS, 128), jnp.int32),
            pltpu.SMEM((SLOTS, 128), jnp.int32),
            dma((SENDS,)),
            dma((GROUPS, 4)),
            dma((GROUPS, 2, 2)),
            dma((2, GROUPS)),
            dma((RB,)),
            dma((RB,)),
            dma((3,)),
        ],
        compiler_params=pltpu.CompilerParams(
            collective_id=0, has_side_effects=True, vmem_limit_bytes=40 << 20
        ),
        name="gather_and_square",
    )(x, x_cols, c_cols, c_keep)


def on_device(x_blocks, x_cols, c_cols, c_keep):
    return square(x_blocks.reshape(RB, BLK, 128), x_cols.T, c_cols.T, c_keep.T)


def solution(mesh):
    spec = P("rows", "section")
    blocks = P("rows", "section", None, None, None)
    return jax.shard_map(
        on_device, mesh=mesh, in_specs=(blocks, spec, spec, spec), out_specs=blocks, check_vma=False
    )
```

time: 123 us -> 120 us (0.976)
  Pallas kernels: 119 us -> 115 us
  local copies, waits for them, and re-layouts: 2.54 us -> 4.56 us
  other arithmetic: 1.36 us -> 0 us
    pallas_call x1, Pallas kernels: 119 us -> 115 us  [square(): pl.pallas_call(square_kernel, out_shape=jax.ShapeDtypeStruct((RB, LC, 2,...]
    unnamed x3 -> x9, local copies, waits for them, and re-layouts: 2.53 us -> 4.56 us
where the time goes in v4:
time: 120 us
  Pallas kernels  115 us (96%)
  local copies, waits for them, and re-layouts  4.56 us (4%)
    pallas_call x1, Pallas kernels, square(): pl.pallas_call(square_kernel, out_shape=jax.ShapeDtypeStruct((RB, LC, 2,...  115 us
    unnamed x9, local copies, waits for them, and re-layouts  4.56 us

profile of v4, /device:TPU:1, one launch (start us, length us, event | category | flops | bytes accessed | tf_op | source)
XLA Modules:
  0.0 119.8 jit_solution(6080690948011935494)
XLA Ops:
  0.0 0.0 copy-start
  0.0 1.1 copy-done
  1.1 0.0 copy-start.1
  1.1 0.7 copy-done.1
  1.8 0.0 copy-start.2
  1.8 0.7 copy-done.2
  2.5 0.0 copy-start.3
  2.5 0.7 copy-done.3
  3.2 115.2 %gather_and_square.1 = bf16[12,3,2,128,128]{4,3,2,1,0:T(8,128)(2,1)S(1)} custom-call(bf16[12,256,128]{2,1,0:T(8,128)(2,1)S(1)} %bitcast.4, s32[1,12]{1,0:T(1,128)S(1)} %bitcast.7, s32[3,12]{1,0:T(4,128)S(1)} %bitcast.5, s32[3,12]{1,0:T(4,128)S(1)} %bitcast.6), custom_call_target="tpu_custom_call" | custom-call | tf_op jit(solution)/shard_map/gather_and_square/pallas_call | solution.py:388
  118.4 1.4 %copy.6 = bf16[12,3,2,128,128]{4,3,2,1,0:T(8,128)(2,1)} copy(bf16[12,3,2,128,128]{4,3,2,1,0:T(8,128)(2,1)S(1)} %gather_and_square.1) | data formatting | bytes 4718592
Async XLA Ops:
  0.0 1.1 copy-start
  1.1 0.7 copy-start.1
  1.8 0.7 copy-start.2
  2.5 0.7 copy-start.3

commit v5 on v4

--- a/solution.py
+++ b/solution.py
@@ -256,6 +256,9 @@
     y_end(home, here, y_first)
     x_sends(home, group(here, y2, 1), y_first)
     ring(2)
+    for unit in x_first:
+        for lo in (0, 1):
+            y_sends(home & beside[lo], group(lo, y, unit[0]), unit)
     for lo in (0, 1):
         y_pass(away, lo, x_first[0])
     for lo in (0, 1):
@@ -264,9 +267,6 @@
         y_pass(home, here, unit)
     for lo in (0, 1):
         x_pass(True, lo, y, y_first)
-    for unit in x_first:
-        for lo in (0, 1):
-            y_sends(home & beside[lo], group(lo, y, unit[0]), unit)
     for lo in (0, 1):
         x_pass(True, lo, ym, y_first)
     for lo in (0, 1):

time: 120 us -> 116 us (0.967)
  Pallas kernels: 115 us -> 111 us
    pallas_call x1, Pallas kernels: 115 us -> 111 us  [square(): pl.pallas_call(square_kernel, out_shape=jax.ShapeDtypeStruct((RB, LC, 2,...]
where the time goes in v5:
time: 116 us
  Pallas kernels  111 us (96%)
  local copies, waits for them, and re-layouts  4.56 us (4%)
    pallas_call x1, Pallas kernels, square(): pl.pallas_call(square_kernel, out_shape=jax.ShapeDtypeStruct((RB, LC, 2,...  111 us
    unnamed x9, local copies, waits for them, and re-layouts  4.56 us

profile of v5, /device:TPU:1, one launch (start us, length us, event | category | flops | bytes accessed | tf_op | source)
XLA Modules:
  0.0 115.6 jit_solution(16793559451653809067)
XLA Ops:
  0.0 0.0 copy-start
  0.0 1.1 copy-done
  1.1 0.0 copy-start.1
  1.1 0.7 copy-done.1
  1.8 0.0 copy-start.2
  1.8 0.7 copy-done.2
  2.5 0.0 copy-start.3
  2.5 0.7 copy-done.3
  3.2 111.0 %gather_and_square.1 = bf16[12,3,2,128,128]{4,3,2,1,0:T(8,128)(2,1)S(1)} custom-call(bf16[12,256,128]{2,1,0:T(8,128)(2,1)S(1)} %bitcast.4, s32[1,12]{1,0:T(1,128)S(1)} %bitcast.7, s32[3,12]{1,0:T(4,128)S(1)} %bitcast.5, s32[3,12]{1,0:T(4,128)S(1)} %bitcast.6), custom_call_target="tpu_custom_call" | custom-call | tf_op jit(solution)/shard_map/gather_and_square/pallas_call | solution.py:388
  114.2 1.4 %copy.6 = bf16[12,3,2,128,128]{4,3,2,1,0:T(8,128)(2,1)} copy(bf16[12,3,2,128,128]{4,3,2,1,0:T(8,128)(2,1)S(1)} %gather_and_square.1) | data formatting | bytes 4718592
Async XLA Ops:
  0.0 1.1 copy-start
  1.1 0.7 copy-start.1
  1.8 0.7 copy-start.2
  2.5 0.7 copy-start.3
